TPU v7x, 256 devices: a whole 4x4x8 slice. The times are simulated.
256 devices in a mesh: strat: 32 (over z, y_hi, core), grp: 8 (over x, y_lo).
Axes of the slice: x: 4, y: 4 (y_hi: 2, y_lo: 2; y = y_hi * 2 + y_lo), z: 8, core: 2. Of those that a mesh axis runs over, the one named last changes fastest.
Arguments:
- user_factors: float32 [262144, 256], P(('strat', 'grp')), may hold values from -1.5 to 1.5
- item_factors: float32 [131072, 256], P('strat'), may hold values from -1.5 to 1.5
- tile_coords: int32 [32, 8, 3, 2, 16], P('strat', 'grp'), may hold values from 0 to 31, as said below
- tile_counts: int32 [32, 8, 3], P('strat', 'grp'), may hold values from 5 to 16, as said below
- tile_values: bfloat16 [32, 8, 3, 16, 128, 128], P('strat', 'grp'), may hold values from 0 to 10
Outputs:
- users_out: float32 [262144, 256], P(('strat', 'grp'))
- items_out: float32 [131072, 256], P('strat')
Inputs may be any that keep to these rules, and one draw needn't show every extreme that they name: `tile_coords`: each list names distinct tiles; user tiles lie below 8 and item tiles below 32; entries at and after the count are ignored. `tile_counts`: in every sub-epoch some device has exactly 16 live tiles.
All inputs are finite; a program needn't handle non-finite values.
Results may differ from a plain program's by a relative error of at most 0.0018.
Values sent between devices are 32-bit elements; how exact they have to be, the bound alone decides.
A program may use at most 64 MiB of HBM per device.

v0:
```python
import jax
import jax.numpy as jnp
from jax import lax
from jax.sharding import PartitionSpec as P


def from_behind(block, axis, distance):
    devices = range(lax.axis_size(axis))
    route = [((i - distance) % len(devices), i) for i in devices]
    return lax.ppermute(block, axis, route)


def tile_terms(user_b, slab_b, coords, count, values):
    high = lax.Precision.HIGHEST
    side = values.shape[-1]
    width = user_b.shape[1]
    user_tiles = user_b.shape[0] // side
    item_tiles = slab_b.shape[0] // side
    urows = jnp.take(user_b.reshape(user_tiles, side, width), coords[0], axis=0)
    irows = jnp.take(slab_b.reshape(item_tiles, side, width), coords[1], axis=0)
    predicted = jnp.einsum("nrk,nck->nrc", urows, irows, preferred_element_type=jnp.float32)
    resid = (values.astype(jnp.float32) - predicted).astype(jnp.bfloat16)
    user_part = jnp.einsum("nrc,nck->nrk", resid, irows, preferred_element_type=jnp.float32)
    item_part = jnp.einsum("nrc,nrk->nck", resid, urows, preferred_element_type=jnp.float32)
    live = jnp.arange(coords.shape[1]) < count
    one_user = ((coords[0][:, None] == jnp.arange(user_tiles)[None, :]) & live[:, None]).astype(
        jnp.float32
    )
    one_item = ((coords[1][:, None] == jnp.arange(item_tiles)[None, :]) & live[:, None]).astype(
        jnp.float32
    )
    user_grad = jnp.einsum("nt,nrk->trk", one_user, user_part, precision=high).reshape(-1, width)
    item_grad = jnp.einsum("nt,nrk->trk", one_item, item_part, precision=high).reshape(-1, width)
    return (user_grad, item_grad)


def per_device(user_factors, item_factors, tile_coords, tile_counts, tile_values):
    users = user_factors
    slab = item_factors
    coords = tile_coords[0, 0]
    counts = tile_counts[0, 0]
    values = tile_values[0, 0]
    rounds = coords.shape[0]
    for sub in range(rounds):
        user_grad, item_grad = tile_terms(
            users.astype(jnp.bfloat16),
            slab.astype(jnp.bfloat16),
            coords[sub],
            counts[sub],
            values[sub],
        )
        users = users - 0.003 * (0.05 * users - user_grad)
        total = lax.psum(item_grad, "grp")
        slab = slab - 0.003 * (0.05 * slab - total)
        if sub + 1 < rounds:
            slab = from_behind(slab, "strat", -1)
    return (users, slab)


def solution(mesh):
    placed = (
        P(("strat", "grp"), None),
        P("strat", None),
        P("strat", "grp", None, None, None),
        P("strat", "grp", None),
        P("strat", "grp", None, None, None, None),
    )
    return jax.shard_map(
        per_device,
        mesh=mesh,
        in_specs=placed,
        out_specs=(P(("strat", "grp"), None), P("strat", None)),
        check_vma=False,
    )
```

profile of v0, /device:TPU:1, one launch (start us, length us, event | category | flops | bytes accessed | tf_op | source)
XLA Modules:
  0.0 752.5 jit_solution(12786251001411020271)
XLA Ops:
  8.8 1.4 fusion.68
  10.8 1.3 convert_element_type.53
  12.1 2.4 convert_element_type.54
  14.5 1.6 gather_fusion
  16.7 2.0 fusion.12
  19.2 2.9 fusion.8
  22.1 4.4 copy.8
  26.6 190.7 %all-reduce.4.cloned.1.call-done = f32[4096,256]{1,0:T(8,128)} async-done(((f32[4096,256]{1,0:T(8,128)}), f32[4096,256]{1,0:T(8,128)}) %all-reduce.4.cloned.1.call-update) | async-done | bytes 4194320 | tf_op jit(solution)/shard_map/psum | solution.py:53
  217.3 6.2 multiply_subtract_fusion.2
  224.8 2.0 fusion.10
  227.3 1.6 gather_fusion.2
  229.5 43.7 %collective-permute-done = f32[4096,256]{1,0:T(8,128)} collective-permute-done((f32[4096,256]{1,0:T(8,128)}, f32[4096,256]{1,0:T(8,128)}, u32[]{:S(2)}, u32[]{:S(2)}) %collective-permute-start) | collective-permute-done | bytes 4194336 | tf_op jit(solution)/shard_map/ppermute | solution.py:10
  273.2 3.7 convert_element_type.59
  276.9 2.2 gather_fusion.3
  279.1 2.0 fusion.13
  281.9 2.9 fusion.4
  284.9 4.4 copy.10
  289.4 188.5 %all-reduce.6.cloned.1.call-done = f32[4096,256]{1,0:T(8,128)} async-done(((f32[4096,256]{1,0:T(8,128)}), f32[4096,256]{1,0:T(8,128)}) %all-reduce.6.cloned.1.call-update) | async-done | bytes 4194320 | tf_op jit(solution)/shard_map/psum | solution.py:53
  477.9 6.2 multiply_subtract_fusion.1
  486.1 2.0 fusion.6
  489.5 2.6 gather_fusion.4
  492.1 41.7 %collective-permute-done.1 = f32[4096,256]{1,0:T(8,128)} collective-permute-done((f32[4096,256]{1,0:T(8,128)}, f32[4096,256]{1,0:T(8,128)}, u32[]{:S(2)}, u32[]{:S(2)}) %collective-permute-start.1) | collective-permute-done | bytes 4194336 | tf_op jit(solution)/shard_map/ppermute | solution.py:10
  533.8 3.7 convert_element_type.64
  537.5 3.3 gather_fusion.5
  540.8 2.3 fusion.14
  543.9 2.9 fusion
  546.8 4.4 copy.12
  551.3 1.9 fusion.26
  553.2 2.0 fusion.2
  555.5 1.4 fusion.16
  556.9 182.9 %all-reduce.8.cloned.1.call-done = f32[4096,256]{1,0:T(8,128)} async-done(((f32[4096,256]{1,0:T(8,128)}), f32[4096,256]{1,0:T(8,128)}) %all-reduce.8.cloned.1.call-update) | async-done | bytes 4194320 | tf_op jit(solution)/shard_map/psum | solution.py:53
  739.8 6.2 multiply_subtract_fusion
  (41 shorter events, 11.3 us)
Async XLA Ops:
  7.2 210.1 %all-reduce.4.cloned.1.call-start = ((), (), s32[]{:S(2)}) async-start(), calls=%async_computation | async-start | bytes 8388608 | tf_op jit(solution)/shard_map/psum | solution.py:53
  16.7 2.0 copy-start.3
  26.6 451.3 %all-reduce.6.cloned.1.call-start = ((), (), s32[]{:S(2)}) async-start(), calls=%async_computation.1 | async-start | bytes 8388608 | tf_op jit(solution)/shard_map/psum | solution.py:53
  223.5 49.8 %collective-permute-start = (f32[4096,256]{1,0:T(8,128)}, f32[4096,256]{1,0:T(8,128)}, u32[]{:S(2)}, u32[]{:S(2)}) collective-permute-start(f32[4096,256]{1,0:T(8,128)} %multiply_subtract_fusion.2), channel_id=1, source_target_pairs={{8,0},{16,8},{24,16},{32,24},{40,32},{48,40},{56,48},{64,56},{72,6... | collective-permute-start | bytes 12582920 | tf_op jit(solution)/shard_map/ppermute | solution.py:10
  224.8 2.4 copy-start
  279.1 2.0 copy-start.1
  281.1 0.8 copy-start.4
  289.3 450.5 %all-reduce.8.cloned.1.call-start = ((), (), s32[]{:S(2)}) async-start(), calls=%async_computation.2 | async-start | bytes 8388608 | tf_op jit(solution)/shard_map/psum | solution.py:53
  477.9 7.7 %copy-start.5 = (bf16[16,128,128]{2,1,0:T(8,128)(2,1)S(1)}, bf16[16,128,128]{2,1,0:T(8,128)(2,1)}, u32[]{:S(2)}) copy-start(bf16[16,128,128]{2,1,0:T(8,128)(2,1)} %copy-done.4) | copy-start | bytes 1572868
  484.1 49.8 %collective-permute-start.1 = (f32[4096,256]{1,0:T(8,128)}, f32[4096,256]{1,0:T(8,128)}, u32[]{:S(2)}, u32[]{:S(2)}) collective-permute-start(f32[4096,256]{1,0:T(8,128)} %multiply_subtract_fusion.1), channel_id=1, source_target_pairs={{8,0},{16,8},{24,16},{32,24},{40,32},{48,40},{56,48},{64,56},{72,6... | collective-permute-start | bytes 12582920 | tf_op jit(solution)/shard_map/ppermute | solution.py:10
  540.8 2.3 copy-start.2
  543.1 0.8 copy-start.6
Sparse Core Ops, SparseCore 0:
  26.7 190.5 all-reduce.3
  289.4 188.3 all-reduce.5
  551.4 188.3 all-reduce.7
where the time goes:
time: 753 us
  waiting for transfers between devices  648 us (86%)
  other arithmetic  34.9 us (5%)
  local copies, waits for them, and re-layouts  28.9 us (4%)
  matrix products  25.3 us (3%)
  between operations  14 us (2%)
    psum x3, waiting for transfers between devices, per_device(): total = lax.psum(item_grad, 'grp')  562 us
    ppermute x2, waiting for transfers between devices, from_behind(): return lax.ppermute(block, axis, route)  85.4 us
    sub x3, other arithmetic, per_device(): slab = slab - 0.003 * (0.05 * slab - total)  18.5 us
  transfers between devices with their start and end apart: 5, of which 5 were waited for; matrix products, arithmetic and copies ran while one was open for 2% of the time, Pallas kernels for 0%

commit v1 on v0

--- a/solution.py
+++ b/solution.py
@@ -50,7 +50,7 @@
             values[sub],
         )
         users = users - 0.003 * (0.05 * users - user_grad)
-        total = lax.psum(item_grad, "grp")
+        total = jnp.sum(lax.all_gather(item_grad, "grp"), axis=0)
         slab = slab - 0.003 * (0.05 * slab - total)
         if sub + 1 < rounds:
             slab = from_behind(slab, "strat", -1)

time: 753 us -> 2170 us (2.88)
  waiting for transfers between devices: 648 us -> 2010 us
  other arithmetic: 34.9 us -> 77.9 us
    all_gather x0 -> x3, waiting for transfers between devices: none -> 1930 us  [per_device(): total = jnp.sum(lax.all_gather(item_grad, 'grp'), axis=0)]
    psum x3 -> x0, waiting for transfers between devices: 562 us -> none  [per_device(): total = lax.psum(item_grad, 'grp')]
    reduce_sum x0 -> x3, other arithmetic: none -> 43 us  [per_device(): total = jnp.sum(lax.all_gather(item_grad, 'grp'), axis=0)]
  transfers between devices with their start and end apart: 5 -> 5, of which waited for: 5 -> 5; matrix products, arithmetic and copies ran while one was open for 2% -> 1% of each run, Pallas kernels for 0% -> 0%
where the time goes in v1:
time: 2170 us; the launch traced here: 2160 us
  waiting for transfers between devices  2010 us (93%)
  other arithmetic  77.9 us (4%)
  local copies, waits for them, and re-layouts  28.9 us (1%)
  matrix products  25.5 us (1%)
    all_gather x3, waiting for transfers between devices, per_device(): total = jnp.sum(lax.all_gather(item_grad, 'grp'), axis=0)  1930 us
    ppermute x2, waiting for transfers between devices, from_behind(): return lax.ppermute(block, axis, route)  85.4 us
  transfers between devices with their start and end apart: 5, of which 5 were waited for; matrix products, arithmetic and copies ran while one was open for 1% of the time, Pallas kernels for 0%

profile of v1, /device:TPU:1, one launch (start us, length us, event | category | flops | bytes accessed | tf_op | source)
XLA Modules:
  0.0 2163.9 jit_solution(13051618496336947924)
XLA Ops:
  12.1 2.4 convert_element_type.54
  14.5 1.6 gather_fusion
  16.7 2.0 fusion.12
  19.2 2.9 fusion.8
  22.1 4.4 copy.17
  26.7 646.5 %all-gather.4.cloned.1.call-done = f32[8,4096,256]{2,1,0:T(8,128)} async-done(((f32[1,4096,256]{2,1,0:T(8,128)}), f32[8,4096,256]{2,1,0:T(8,128)}) %all-gather.4.cloned.1.call-update) | async-done | bytes 33554448 | tf_op jit(solution)/shard_map/all_gather | solution.py:53
  673.1 14.3 reduce_sum.27
  687.5 6.2 multiply_subtract_fusion.2
  695.4 2.0 fusion.10
  698.0 1.6 gather_fusion.2
  700.2 43.6 %collective-permute-done = f32[4096,256]{1,0:T(8,128)} collective-permute-done((f32[4096,256]{1,0:T(8,128)}, f32[4096,256]{1,0:T(8,128)}, u32[]{:S(2)}, u32[]{:S(2)}) %collective-permute-start) | collective-permute-done | bytes 4194336 | tf_op jit(solution)/shard_map/ppermute | solution.py:10
  743.8 3.7 convert_element_type.59
  747.5 2.2 gather_fusion.3
  749.7 2.0 fusion.13
  752.5 2.9 fusion.4
  755.5 4.4 copy.22
  760.0 644.4 %all-gather.6.cloned.1.call-done = f32[8,4096,256]{2,1,0:T(8,128)} async-done(((f32[1,4096,256]{2,1,0:T(8,128)}), f32[8,4096,256]{2,1,0:T(8,128)}) %all-gather.6.cloned.1.call-update) | async-done | bytes 33554448 | tf_op jit(solution)/shard_map/all_gather | solution.py:53
  1404.4 14.3 reduce_sum.28
  1418.7 6.2 multiply_subtract_fusion.1
  1427.0 2.0 fusion.6
  1430.4 2.6 gather_fusion.4
  1433.0 41.8 %collective-permute-done.1 = f32[4096,256]{1,0:T(8,128)} collective-permute-done((f32[4096,256]{1,0:T(8,128)}, f32[4096,256]{1,0:T(8,128)}, u32[]{:S(2)}, u32[]{:S(2)}) %collective-permute-start.1) | collective-permute-done | bytes 4194336 | tf_op jit(solution)/shard_map/ppermute | solution.py:10
  1474.8 3.7 convert_element_type.64
  1478.5 3.2 gather_fusion.5
  1481.7 2.3 fusion.14
  1484.8 2.9 fusion
  1487.7 4.4 copy.27
  1492.2 1.9 fusion.26
  1494.1 2.2 fusion.2
  1498.0 638.6 %all-gather.8.cloned.1.call-done = f32[8,4096,256]{2,1,0:T(8,128)} async-done(((f32[1,4096,256]{2,1,0:T(8,128)}), f32[8,4096,256]{2,1,0:T(8,128)}) %all-gather.8.cloned.1.call-update) | async-done | bytes 33554448 | tf_op jit(solution)/shard_map/all_gather | solution.py:53
  2136.6 14.3 reduce_sum.29
  2151.0 6.2 multiply_subtract_fusion
  (44 shorter events, 15.9 us)
Async XLA Ops:
  7.2 666.0 %all-gather.4.cloned.1.call-start = ((), (), s32[]{:S(2)}) async-start(), calls=%async_computation | async-start | bytes 37748736 | tf_op jit(solution)/shard_map/all_gather | solution.py:53
  16.7 2.0 copy-start.3
  26.6 1377.8 %all-gather.6.cloned.1.call-start = ((), (), s32[]{:S(2)}) async-start(), calls=%async_computation.1 | async-start | bytes 37748736 | tf_op jit(solution)/shard_map/all_gather | solution.py:53
  693.6 50.2 %collective-permute-start = (f32[4096,256]{1,0:T(8,128)}, f32[4096,256]{1,0:T(8,128)}, u32[]{:S(2)}, u32[]{:S(2)}) collective-permute-start(f32[4096,256]{1,0:T(8,128)} %multiply_subtract_fusion.2), channel_id=1, source_target_pairs={{8,0},{16,8},{24,16},{32,24},{40,32},{48,40},{56,48},{64,56},{72,6... | collective-permute-start | bytes 12582920 | tf_op jit(solution)/shard_map/ppermute | solution.py:10
  695.4 2.4 copy-start
  749.7 2.0 copy-start.1
  751.7 0.8 copy-start.4
  759.9 1376.7 %all-gather.8.cloned.1.call-start = ((), (), s32[]{:S(2)}) async-start(), calls=%async_computation.2 | async-start | bytes 37748736 | tf_op jit(solution)/shard_map/all_gather | solution.py:53
  1418.7 7.8 copy-start.5
  1424.9 49.9 %collective-permute-start.1 = (f32[4096,256]{1,0:T(8,128)}, f32[4096,256]{1,0:T(8,128)}, u32[]{:S(2)}, u32[]{:S(2)}) collective-permute-start(f32[4096,256]{1,0:T(8,128)} %multiply_subtract_fusion.1), channel_id=1, source_target_pairs={{8,0},{16,8},{24,16},{32,24},{40,32},{48,40},{56,48},{64,56},{72,6... | collective-permute-start | bytes 12582920 | tf_op jit(solution)/shard_map/ppermute | solution.py:10
  1481.7 2.3 copy-start.2
  1484.0 0.8 copy-start.6
Sparse Core Ops, SparseCore 0:
  26.7 646.3 all-gather.3
  760.0 644.2 all-gather.5
  1492.3 644.2 all-gather.7
